TPU v7x, 256 devices: a whole 4x4x8 slice. The times are simulated.
256 devices in a mesh: mem: 16 (over x_hi, y, core), tile: 16 (over x_lo, z).
Axes of the slice: x: 4 (x_hi: 2, x_lo: 2; x = x_hi * 2 + x_lo), y: 4, z: 8, core: 2. Of those that a mesh axis runs over, the one named last changes fastest.
Arguments:
- alpha: bfloat16 [16, 16, 720, 1440], P('mem', None, 'tile'), may hold values from -6 to 6
- perturbation: bfloat16 [16, 16, 720, 1440], P('mem', None, 'tile'), may hold values from -3 to 3
- lon_scale: float32 [16], replicated, may hold values from 8 to 48
- lat_scale: float32 [16], replicated, may hold values from 12 to 64
- obs_level: int32 [16, 16384], P('tile'), may hold values from 0 to 15
- obs_row: int32 [16, 16384], P('tile'), may hold values from 0 to 44
- obs_col: int32 [16, 16384], P('tile'), may hold values from 0 to 1439
- obs_count: int32 [16], P('tile'), may hold values from 8192 to 16384, as said below
- innovation: float32 [16, 16384], P('tile'), may hold values from -12 to 12
- obs_weight: float32 [16, 16384], P('tile'), may hold values from 1 to 8
Outputs:
- gradient: bfloat16 [16, 16, 720, 1440], P('mem', None, 'tile')
Inputs may be any that keep to these rules, and one draw needn't show every extreme that they name: Observations of band t fill slots 0 to obs_count[t] - 1; the other slots carry no observation. Some band is full in every draw.
All inputs are finite; a program needn't handle non-finite values.
Results may differ from a plain program's by a relative error of at most 0.0056.
Values may be sent and summed in bfloat16 or wider, within the bound.
No kernel may reach another device: no remote copies, remote signals or barrier semaphores. Data moves between devices by JAX's collectives and lax.ppermute only.
A program may use at most 128 MiB of HBM per device.

v0:
```python
import jax
import jax.numpy as jnp
from jax import lax
from jax.sharding import PartitionSpec as P


def square_root(lengths, extent, periodic):
    positions = jnp.arange(extent).astype(jnp.float32)
    distance = jnp.abs(positions[:, None] - positions[None, :])
    if periodic:
        distance = jnp.minimum(distance, extent - distance)
    scales = lengths[:, None, None]
    factor = (2.0 / jnp.pi) ** 0.25
    values = factor * jnp.exp(-((distance[None] / scales) ** 2)) / jnp.sqrt(scales)
    return values.astype(jnp.bfloat16)


def localize(values_in, lat_root, lon_root):
    zonal = jnp.einsum(
        "klab,lbc->klac", values_in, lon_root, preferred_element_type=jnp.float32
    ).astype(jnp.bfloat16)
    return jnp.einsum("lab,klbc->klac", lat_root, zonal, preferred_element_type=jnp.float32)


def pick_cells(flat_rows, row_place, column):
    slots = row_place.shape[0]
    block = min(4096, slots)
    width = flat_rows.shape[1]
    counter = jnp.arange(width)

    def pick_one_block(pair):
        rows_here, cols_here = pair
        taken = flat_rows[rows_here]
        return jnp.sum(jnp.where(counter[None, :] == cols_here[:, None], taken, 0.0), axis=1)

    picked = lax.map(pick_one_block, (row_place.reshape(-1, block), column.reshape(-1, block)))
    return picked.reshape(-1)


def place_cells(row_total, width, row_place, column, values):
    slots = row_place.shape[0]
    block = min(4096, slots)
    counter = jnp.arange(width)

    def place_one_block(field, triple):
        rows_here, cols_here, vals_here = triple
        lines = jnp.where(counter[None, :] == cols_here[:, None], vals_here[:, None], 0.0)
        return (field.at[rows_here].add(lines, mode="drop"), jnp.float32(0.0))

    start_field = jnp.zeros((row_total, width), jnp.float32)
    triples = (row_place.reshape(-1, block), column.reshape(-1, block), values.reshape(-1, block))
    return lax.scan(place_one_block, start_field, triples)[0]


def shards(
    alpha,
    perturbation,
    lon_scale,
    lat_scale,
    obs_level,
    obs_row,
    obs_col,
    obs_count,
    innovation,
    obs_weight,
):
    level_count = alpha.shape[1]
    row_count = alpha.shape[2]
    column_count = alpha.shape[3]
    tile_count = lax.axis_size("tile")
    tile_index = lax.axis_index("tile")
    slab_levels = level_count // tile_count
    first_level = tile_index * slab_levels
    lon_part = lax.dynamic_slice_in_dim(lon_scale, first_level, slab_levels)
    lat_part = lax.dynamic_slice_in_dim(lat_scale, first_level, slab_levels)
    lon_root = square_root(lon_part, column_count, True)
    lat_root = square_root(lat_part, row_count * tile_count, False)
    level_index = obs_level[0]
    row_index = obs_row[0]
    column = obs_col[0]
    slot_count = obs_level.shape[1]
    valid = jnp.arange(slot_count) < obs_count[0]
    band_line = level_index * row_count + row_index
    alpha_slab = lax.all_to_all(alpha, "tile", split_axis=1, concat_axis=2, tiled=True)
    spread_slab = localize(alpha_slab, lat_root, lon_root).astype(jnp.bfloat16)
    spread_band = lax.all_to_all(spread_slab, "tile", split_axis=2, concat_axis=1, tiled=True)
    partial_field = jnp.sum(
        perturbation.astype(jnp.float32) * spread_band.astype(jnp.float32), axis=0
    )
    total_field = lax.psum(partial_field, "mem")
    model_obs = pick_cells(total_field.reshape(-1, column_count), band_line, column)
    weighted = jnp.where(valid, obs_weight[0] * (model_obs - innovation[0]), 0.0)
    obs_field = place_cells(level_count * row_count, column_count, band_line, column, weighted)
    obs_field = obs_field.reshape(level_count, row_count, column_count)
    sensitive = (perturbation.astype(jnp.float32) * obs_field[None]).astype(jnp.bfloat16)
    sensitive_slab = lax.all_to_all(sensitive, "tile", split_axis=1, concat_axis=2, tiled=True)
    gradient_slab = (
        alpha_slab.astype(jnp.float32) + localize(sensitive_slab, lat_root, lon_root)
    ).astype(jnp.bfloat16)
    return lax.all_to_all(gradient_slab, "tile", split_axis=2, concat_axis=1, tiled=True)


def solution(mesh):
    in_specs = (
        P("mem", None, "tile", None),
        P("mem", None, "tile", None),
        P(),
        P(),
        P("tile", None),
        P("tile", None),
        P("tile", None),
        P("tile"),
        P("tile", None),
        P("tile", None),
    )
    out_specs = P("mem", None, "tile", None)
    return jax.shard_map(shards, mesh=mesh, in_specs=in_specs, out_specs=out_specs, check_vma=False)
```

profile of v0, /device:TPU:34, one launch (start us, length us, event | category | flops | bytes accessed | tf_op | source)
XLA Modules:
  0.0 922.1 jit_solution(17614433650385890455)
XLA Ops:
  23.2 50.1 %all-to-all-done = bf16[1,16,45,1440]{3,2,0,1:T(8,128)(2,1)S(1)} async-done(((bf16[1,16,45,1440]{3,2,0,1:T(8,128)(2,1)}), bf16[1,16,45,1440]{3,2,0,1:T(8,128)(2,1)S(1)}, u32[]{:S(2)}, u32[]{:S(2)}) %all-to-all-start) | async-done | bytes 2073632 | tf_op jit(solution)/shard_map/all_to_all | solution.py:84
  75.5 11.9 %fusion.29 = bf16[1,1,720,1440]{2,3,0,1:T(8,128)(2,1)} fusion(bf16[720,1440]{1,0:T(8,128)(2,1)} %reshape.399, f32[]{:T(128)} %bitcast.1, f32[]{:T(128)} %bitcast, f32[1440]{0:T(1024)S(1)} %iota_convert_fusion, f32[]{:T(128)} %bitcast.8, f32[]{:T(128)} %bitcast.7, f32[720]{0:T(1024)S(1)} %iota_convert_fusion.1), kind=kOutput, calls=%fused_computation.37 | convolution fusion | flops 4505932800 | bytes 4155856 | tf_op jit(solution)/shard_map/lab,klbc->klac/dot_general | solution.py:22
  87.3 12.1 %copy.33 = bf16[1,1,720,1440]{3,0,1,2:T(2,128)(2,1)} copy(bf16[1,1,720,1440]{2,3,0,1:T(8,128)(2,1)} %fusion.29) | data formatting | bytes 4147200 | tf_op jit(solution)/shard_map/convert_element_type | solution.py:85
  99.9 13.8 %reduce.18 = bf16[720,1440]{1,0:T(8,128)(2,1)S(1)} reduce(bf16[720,1,1,1440]{3,2,1,0:T(2,128)(2,1)} %bitcast.101, bf16[]{:T(256)} %broadcast.349), dimensions={1,2}, to_apply=%bitcast.69.reduce_sub_computation | reduce | bytes 4147202
  119.0 56.9 %all_to_all.19 = bf16[16,2,32400]{2,1,0:T(2,128)(2,1)S(1)} all-to-all(bf16[16,2,32400]{2,1,0:T(2,128)(2,1)} %reshape.462), channel_id=1, replica_groups=mesh['mem'=16,'tile'=16] {'tile'}, dimensions={0} | all-to-all | bytes 4147200 | tf_op jit(solution)/shard_map/all_to_all | solution.py:86
  211.8 147.9 %all-reduce.2.cloned.1.call-done = f32[720,1440]{1,0:T(8,128)} async-done(((f32[720,1440]{1,0:T(8,128)}), f32[720,1440]{1,0:T(8,128)}) %all-reduce.2.cloned.1.call-update) | async-done | bytes 4147216 | tf_op jit(solution)/shard_map/psum | solution.py:90
  359.7 162.5 %while.24 = (s32[]{:T(128)}, f32[4,4096]{1,0:T(4,128)S(1)}, s32[4,4096]{1,0:T(4,128)S(1)}, s32[4,4096]{1,0:T(4,128)S(1)}, f32[720,1440]{1,0:T(8,128)}) while((s32[]{:T(128)}, f32[4,4096]{1,0:T(4,128)S(1)}, s32[4,4096]{1,0:T(4,128)S(1)}, s32[4,4096]{1,0:T(4,128)S(1)}, f32[720,1440]{1,0:T(8,128)}) %tuple.43), condition=%wide.region_3.4_spmd.clone.clone, body=%wide.region_1.3_spmd.clone.sunk.clone | while | flops 17707008 | bytes 70959168 | solution.py:36
  359.8 29.5 %gather_fusion = f32[4096,1440]{1,0:T(8,128)} fusion(f32[720,1440]{1,0:T(8,128)} %get-tuple-element.217, s32[4096]{0:T(1024)S(1)} %broadcast_clamp_fusion.3), kind=kCustom, calls=%fused_computation.clone.clone.1.clone | custom fusion | bytes 47202304 | tf_op jit(solution)/shard_map/while/body/eval_jaxpr/gather | solution.py:33
  389.3 10.8 %select_reduce_fusion.3 = f32[4096]{0:T(1024)S(1)} fusion(f32[4096,1440]{1,0:T(8,128)} %gather_fusion, s32[4096]{0:T(1024)S(1)} %bitcast.107), kind=kLoop, calls=%fused_computation.5.clone.1.clone | loop fusion | flops 17690624 | bytes 23625728 | tf_op jit(solution)/shard_map/while/body/eval_jaxpr/reduce_sum | solution.py:34
  400.4 29.4 %gather_fusion = f32[4096,1440]{1,0:T(8,128)} fusion(f32[720,1440]{1,0:T(8,128)} %get-tuple-element.217, s32[4096]{0:T(1024)S(1)} %broadcast_clamp_fusion.3), kind=kCustom, calls=%fused_computation.clone.clone.1.clone | custom fusion | bytes 47202304 | tf_op jit(solution)/shard_map/while/body/eval_jaxpr/gather | solution.py:33
  440.9 29.4 %gather_fusion = f32[4096,1440]{1,0:T(8,128)} fusion(f32[720,1440]{1,0:T(8,128)} %get-tuple-element.217, s32[4096]{0:T(1024)S(1)} %broadcast_clamp_fusion.3), kind=kCustom, calls=%fused_computation.clone.clone.1.clone | custom fusion | bytes 47202304 | tf_op jit(solution)/shard_map/while/body/eval_jaxpr/gather | solution.py:33
  481.5 29.4 %gather_fusion = f32[4096,1440]{1,0:T(8,128)} fusion(f32[720,1440]{1,0:T(8,128)} %get-tuple-element.217, s32[4096]{0:T(1024)S(1)} %broadcast_clamp_fusion.3), kind=kCustom, calls=%fused_computation.clone.clone.1.clone | custom fusion | bytes 47202304 | tf_op jit(solution)/shard_map/while/body/eval_jaxpr/gather | solution.py:33
  511.0 10.8 %select_reduce_fusion.3 = f32[4096]{0:T(1024)S(1)} fusion(f32[4096,1440]{1,0:T(8,128)} %gather_fusion, s32[4096]{0:T(1024)S(1)} %bitcast.107), kind=kLoop, calls=%fused_computation.5.clone.1.clone | loop fusion | flops 17690624 | bytes 23625728 | tf_op jit(solution)/shard_map/while/body/eval_jaxpr/reduce_sum | solution.py:34
  524.9 188.8 %while.25 = (s32[]{:T(128)}, f32[720,1440]{1,0:T(8,128)}, s32[4,4096]{1,0:T(4,128)S(1)}, s32[4,4096]{1,0:T(4,128)S(1)}, f32[4,4096]{1,0:T(4,128)S(1)}) while((s32[]{:T(128)}, f32[720,1440]{1,0:T(8,128)}, s32[4,4096]{1,0:T(4,128)S(1)}, s32[4,4096]{1,0:T(4,128)S(1)}, f32[4,4096]{1,0:T(4,128)S(1)}) %tuple.52), condition=%wide.region_6.7_spmd.clone.clone, body=%wide.region_4.6_spmd.clone.sunk.clone | while | flops 17707008 | bytes 4278857 | solution.py:52
  525.0 47.1 %scatter_custom_fusion.8 = f32[720,1440]{1,0:T(8,128)} fusion(f32[720,1440]{1,0:T(8,128)} %get-tuple-element.224, s32[4096]{0:T(1024)S(1)} %bitcast.109, f32[]{:T(128)} %constant.35.clone.1..sunk.1, f32[4096]{0:T(1024)S(1)} %bitcast.105, s32[4096]{0:T(1024)S(1)} %bitcast.106), kind=kCustom, calls=%fused_computation.10.clone.1.clone | custom fusion | flops 17694720 | bytes 4180480 | tf_op jit(solution)/shard_map/while/body/eval_jaxpr/scatter-add | solution.py:48
  572.2 47.1 %scatter_custom_fusion.8 = f32[720,1440]{1,0:T(8,128)} fusion(f32[720,1440]{1,0:T(8,128)} %get-tuple-element.224, s32[4096]{0:T(1024)S(1)} %bitcast.109, f32[]{:T(128)} %constant.35.clone.1..sunk.1, f32[4096]{0:T(1024)S(1)} %bitcast.105, s32[4096]{0:T(1024)S(1)} %bitcast.106), kind=kCustom, calls=%fused_computation.10.clone.1.clone | custom fusion | flops 17694720 | bytes 4180480 | tf_op jit(solution)/shard_map/while/body/eval_jaxpr/scatter-add | solution.py:48
  619.4 47.1 %scatter_custom_fusion.8 = f32[720,1440]{1,0:T(8,128)} fusion(f32[720,1440]{1,0:T(8,128)} %get-tuple-element.224, s32[4096]{0:T(1024)S(1)} %bitcast.109, f32[]{:T(128)} %constant.35.clone.1..sunk.1, f32[4096]{0:T(1024)S(1)} %bitcast.105, s32[4096]{0:T(1024)S(1)} %bitcast.106), kind=kCustom, calls=%fused_computation.10.clone.1.clone | custom fusion | flops 17694720 | bytes 4180480 | tf_op jit(solution)/shard_map/while/body/eval_jaxpr/scatter-add | solution.py:48
  666.6 47.1 %scatter_custom_fusion.8 = f32[720,1440]{1,0:T(8,128)} fusion(f32[720,1440]{1,0:T(8,128)} %get-tuple-element.224, s32[4096]{0:T(1024)S(1)} %bitcast.109, f32[]{:T(128)} %constant.35.clone.1..sunk.1, f32[4096]{0:T(1024)S(1)} %bitcast.105, s32[4096]{0:T(1024)S(1)} %bitcast.106), kind=kCustom, calls=%fused_computation.10.clone.1.clone | custom fusion | flops 17694720 | bytes 4180480 | tf_op jit(solution)/shard_map/while/body/eval_jaxpr/scatter-add | solution.py:48
  741.6 12.2 %copy.38 = f32[1,1,720,1440]{2,3,0,1:T(8,128)} copy(f32[1,1,720,1440]{3,0,2,1:T(1,128)} %reshape.405) | data formatting | bytes 8294400 | tf_op jit(solution)/shard_map/convert_element_type | solution.py:98
  753.8 32.6 %all-to-all-done.2 = bf16[1,16,45,1440]{3,2,0,1:T(8,128)(2,1)} async-done(((bf16[1,16,45,1440]{3,2,0,1:T(8,128)(2,1)}), bf16[1,16,45,1440]{3,2,0,1:T(8,128)(2,1)}, u32[]{:S(2)}, u32[]{:S(2)}) %all-to-all-start.2) | async-done | bytes 2073632 | tf_op jit(solution)/shard_map/all_to_all | solution.py:96
  789.8 11.8 %fusion.18 = bf16[1,1,720,1440]{2,3,0,1:T(8,128)(2,1)S(1)} fusion(f32[1,1,720,1440]{2,3,0,1:T(8,128)} %copy.38, bf16[720,1440]{1,0:T(8,128)(2,1)} %reshape.402, f32[]{:T(128)} %bitcast.1, f32[]{:T(128)} %bitcast, f32[1440]{0:T(1024)S(1)} %copy-done.12, f32[]{:T(128)} %bitcast.8, f32[]{:T(128)} %bitcast.7, f32[720]{0:T(1024)S(1)} %copy-done.14), kind=kOutput, calls=%fused_computation.31 | convolution fusion | flops 4506969600 | bytes 8303056 | tf_op jit(solution)/shard_map/lab,klbc->klac/dot_general | solution.py:22
  810.9 14.0 %reduce.19 = bf16[720,1440]{1,0:T(8,128)(2,1)S(1)} reduce(bf16[720,1,1,1440]{3,2,1,0:T(2,128)(2,1)} %bitcast.102, bf16[]{:T(256)} %broadcast.349), dimensions={1,2}, to_apply=%bitcast.71.reduce_sub_computation | reduce | bytes 4147202
  830.0 56.5 %all_to_all.40 = bf16[16,2,32400]{2,1,0:T(2,128)(2,1)S(1)} all-to-all(bf16[16,2,32400]{2,1,0:T(2,128)(2,1)} %reshape.464), channel_id=1, replica_groups=mesh['mem'=16,'tile'=16] {'tile'}, dimensions={0} | all-to-all | bytes 4147200 | tf_op jit(solution)/shard_map/all_to_all | solution.py:100
  895.2 15.3 %bitcast_reduce_fusion = bf16[720,1440]{1,0:T(8,128)(2,1)} fusion(bf16[720,1,1,1440]{3,2,1,0:T(2,128)(2,1)} %reshape.465), kind=kLoop, calls=%fused_computation.51 | loop fusion | bytes 4147200 | tf_op jit(solution)/shard_map/all_to_all | solution.py:100
  (104 shorter events, 142.8 us)
Async XLA Ops:
  6.5 13.8 %copy-start.15 = (f32[16]{0:T(128)S(1)}, f32[16]{0:T(128)}, u32[]{:S(2)}) copy-start(f32[16]{0:T(128)} %param.16) | copy-start | bytes 196
  6.5 15.2 %copy-start.16 = (f32[16]{0:T(128)S(1)}, f32[16]{0:T(128)}, u32[]{:S(2)}) copy-start(f32[16]{0:T(128)} %param.17) | copy-start | bytes 196
  10.8 62.5 %all-to-all-start = ((bf16[1,16,45,1440]{3,2,0,1:T(8,128)(2,1)}), bf16[1,16,45,1440]{3,2,0,1:T(8,128)(2,1)S(1)}, u32[]{:S(2)}, u32[]{:S(2)}) async-start(bf16[1,16,45,1440]{3,2,0,1:T(8,128)(2,1)} %copy.32), calls=%async_computation | async-start | bytes 4718592 | tf_op jit(solution)/shard_map/all_to_all | solution.py:84
  20.3 339.4 %all-reduce.2.cloned.1.call-start = ((), (), s32[]{:S(2)}) async-start(), calls=%async_computation.4 | async-start | bytes 8847360 | tf_op jit(solution)/shard_map/psum | solution.py:90
  23.2 64.2 %copy-start.13 = (f32[720]{0:T(1024)}, f32[720]{0:T(1024)S(1)}, u32[]{:S(2)}) copy-start(f32[720]{0:T(1024)S(1)} %iota_convert_fusion.1) | copy-start | bytes 8644
  23.2 64.1 %copy-start.11 = (f32[1440]{0:T(1024)}, f32[1440]{0:T(1024)S(1)}, u32[]{:S(2)}) copy-start(f32[1440]{0:T(1024)S(1)} %iota_convert_fusion) | copy-start | bytes 17284
  73.3 14.0 %copy-start = (bf16[1,16,45,1440]{3,2,0,1:T(8,128)(2,1)}, bf16[1,16,45,1440]{3,2,0,1:T(8,128)(2,1)S(1)}, u32[]{:S(2)}) copy-start(bf16[1,16,45,1440]{3,2,0,1:T(8,128)(2,1)S(1)} %all-to-all-done) | copy-start | bytes 6220804
  184.7 9.0 copy-start.2
  205.6 0.8 copy-start.8
  205.7 1.7 copy-start.6
  205.7 1.7 copy-start.7
  205.7 2.5 copy-start.9
  205.7 4.0 copy-start.10
  359.7 162.5 %copy-start.4 = (f32[4,4096]{1,0:T(4,128)S(1)}, f32[4,4096]{1,0:T(4,128)}, u32[]{:S(2)}) copy-start(f32[4,4096]{1,0:T(4,128)} %squeeze.23) | copy-start | bytes 196612
  359.7 162.5 %copy-start.5 = (f32[4,4096]{1,0:T(4,128)S(1)}, f32[4,4096]{1,0:T(4,128)}, u32[]{:S(2)}) copy-start(f32[4,4096]{1,0:T(4,128)} %squeeze.24) | copy-start | bytes 196612
  713.7 4.2 copy-start.3
  722.7 11.7 %copy-start.1 = (bf16[1,16,45,1440]{3,2,0,1:T(8,128)(2,1)S(1)}, bf16[1,16,45,1440]{3,2,0,1:T(8,128)(2,1)}, u32[]{:S(2)}) copy-start(bf16[1,16,45,1440]{3,2,0,1:T(8,128)(2,1)} %copy-done) | copy-start | bytes 6220804
  725.4 61.0 %all-to-all-start.2 = ((bf16[1,16,45,1440]{3,2,0,1:T(8,128)(2,1)}), bf16[1,16,45,1440]{3,2,0,1:T(8,128)(2,1)}, u32[]{:S(2)}, u32[]{:S(2)}) async-start(bf16[1,16,45,1440]{3,2,0,1:T(8,128)(2,1)} %copy.37), calls=%async_computation.2 | async-start | bytes 4718592 | tf_op jit(solution)/shard_map/all_to_all | solution.py:96
  753.8 35.9 %copy-start.12 = (f32[1440]{0:T(1024)S(1)}, f32[1440]{0:T(1024)}, u32[]{:S(2)}) copy-start(f32[1440]{0:T(1024)} %copy-done.11) | copy-start | bytes 17284
  753.8 35.9 %copy-start.14 = (f32[720]{0:T(1024)S(1)}, f32[720]{0:T(1024)}, u32[]{:S(2)}) copy-start(f32[720]{0:T(1024)} %copy-done.13) | copy-start | bytes 8644
Sparse Core Ops, SparseCore 0:
  205.8 153.8 all-reduce.1
where the time goes:
time: 932 us; the launch traced here: 922 us
  other arithmetic  279 us (30%)
  local copies, waits for them, and re-layouts  240 us (26%)
  waiting for transfers between devices  231 us (25%)
  blocking collectives  113 us (12%)
  matrix products  23.7 us (3%)
  starting transfers between devices  18.5 us (2%)
  between operations  15.9 us (2%)
    scatter-add x4, other arithmetic, place_one_block(): return (field.at[rows_here].add(lines, mode='drop'), jnp.float32(0.0))  188 us
    psum x1, waiting for transfers between devices, shards(): total_field = lax.psum(partial_field, 'mem')  148 us
    gather x4, local copies, waits for them, and re-layouts, pick_one_block(): taken = flat_rows[rows_here]  118 us
    all_to_all x1, blocking collectives, shards(): lax.all_to_all(spread_slab, 'tile', split_axis=2, concat_axis=1, tiled=True)  56.9 us
    all_to_all x1, blocking collectives, shards(): lax.all_to_all(gradient_slab, 'tile', split_axis=2, concat_axis=1, tiled=...  56.5 us
    all_to_all x1, waiting for transfers between devices, shards(): lax.all_to_all(alpha, 'tile', split_axis=1, concat_axis=2, tiled=True)  50.1 us
    reduce_sum x4, other arithmetic, pick_one_block(): jnp.sum(jnp.where(counter[None, :] == cols_here[:, None], taken, 0.0), ax...  43.1 us
    unnamed x42, local copies, waits for them, and re-layouts  34 us
  transfers between devices with their start and end apart: 3, of which 3 were waited for; matrix products, arithmetic and copies ran while one was open for 3% of the time, Pallas kernels for 0%

commit v1 on v0

--- a/solution.py
+++ b/solution.py
@@ -83,7 +83,12 @@
     band_line = level_index * row_count + row_index
     alpha_slab = lax.all_to_all(alpha, "tile", split_axis=1, concat_axis=2, tiled=True)
     spread_slab = localize(alpha_slab, lat_root, lon_root).astype(jnp.bfloat16)
-    spread_band = lax.all_to_all(spread_slab, "tile", split_axis=2, concat_axis=1, tiled=True)
+    spread_band = jnp.concatenate(
+        lax.all_to_all(
+            jnp.stack(jnp.split(spread_slab, lax.axis_size("tile"), axis=2)), "tile", 0, 0
+        ),
+        axis=1,
+    )
     partial_field = jnp.sum(
         perturbation.astype(jnp.float32) * spread_band.astype(jnp.float32), axis=0
     )

time: 932 us -> 892 us (0.957)
  local copies, waits for them, and re-layouts: 240 us -> 215 us
  other arithmetic: 279 us -> 257 us
    convert_element_type x2 -> x0, local copies, waits for them, and re-layouts: 14.8 us -> none  [the longest x1 12.1 us: shards(): spread_slab = localize(alpha_slab, lat_root, lon_root).astype(jnp.bfloat16)]
    unnamed x5 -> x4, other arithmetic: 30.3 us -> 16.5 us
    unnamed x42 -> x57, local copies, waits for them, and re-layouts: 34 us -> 28 us
where the time goes in v1:
time: 892 us; the launch traced here: 882 us
  other arithmetic  257 us (29%)
  waiting for transfers between devices  231 us (26%)
  local copies, waits for them, and re-layouts  215 us (24%)
  blocking collectives  120 us (13%)
  matrix products  24.6 us (3%)
  starting transfers between devices  18.5 us (2%)
  between operations  15.9 us (2%)
    scatter-add x4, other arithmetic, place_one_block(): return (field.at[rows_here].add(lines, mode='drop'), jnp.float32(0.0))  188 us
    psum x1, waiting for transfers between devices, shards(): total_field = lax.psum(partial_field, 'mem')  148 us
    gather x4, local copies, waits for them, and re-layouts, pick_one_block(): taken = flat_rows[rows_here]  118 us
    all_to_all x1, blocking collectives, shards(): lax.all_to_all(jnp.stack(jnp.split(spread_slab, lax.axis_size('tile'), ax...  63.5 us
    all_to_all x1, blocking collectives, shards(): lax.all_to_all(gradient_slab, 'tile', split_axis=2, concat_axis=1, tiled=...  56.5 us
    all_to_all x1, waiting for transfers between devices, shards(): lax.all_to_all(alpha, 'tile', split_axis=1, concat_axis=2, tiled=True)  50.3 us
    reduce_sum x4, other arithmetic, pick_one_block(): jnp.sum(jnp.where(counter[None, :] == cols_here[:, None], taken, 0.0), ax...  43.1 us
    all_to_all x1, waiting for transfers between devices, shards(): lax.all_to_all(sensitive, 'tile', split_axis=1, concat_axis=2, tiled=True)  32.7 us
  transfers between devices with their start and end apart: 3, of which 3 were waited for; matrix products, arithmetic and copies ran while one was open for 3% of the time, Pallas kernels for 0%

profile of v1, /device:TPU:34, one launch (start us, length us, event | category | flops | bytes accessed | tf_op | source)
XLA Modules:
  0.0 882.2 jit_solution(3734970085583548676)
XLA Ops:
  23.1 50.3 %all-to-all-done = bf16[1,16,45,1440]{3,2,0,1:T(8,128)(2,1)S(1)} async-done(((bf16[1,16,45,1440]{3,2,0,1:T(8,128)(2,1)}), bf16[1,16,45,1440]{3,2,0,1:T(8,128)(2,1)S(1)}, u32[]{:S(2)}, u32[]{:S(2)}) %all-to-all-start) | async-done | bytes 2073632 | tf_op jit(solution)/shard_map/all_to_all | solution.py:84
  75.6 12.9 %convolution_convert_fusion = bf16[1440,720]{0,1:T(8,128)(2,1)} fusion(bf16[720,1440]{1,0:T(8,128)(2,1)} %reshape.397, f32[]{:T(128)} %bitcast.1, f32[]{:T(128)} %bitcast, f32[1440]{0:T(1024)S(1)} %iota_convert_fusion, f32[]{:T(128)} %bitcast.8, f32[]{:T(128)} %bitcast.7, f32[720]{0:T(1024)S(1)} %iota_convert_fusion.1), kind=kOutput, calls=%fused_computation.36 | convolution fusion | flops 4505932800 | bytes 4155856 | tf_op jit(solution)/shard_map/lab,klbc->klac/dot_general | solution.py:22
  96.7 63.5 %all_to_all.35 = bf16[16,1,1,45,1440]{4,3,2,1,0:T(8,128)(2,1)S(1)} all-to-all(bf16[16,1,1,45,1440]{4,3,2,1,0:T(8,128)(2,1)S(1)} %fusion.43), channel_id=1, replica_groups=mesh['mem'=16,'tile'=16] {'tile'}, dimensions={0} | all-to-all | bytes 4147200 | tf_op jit(solution)/shard_map/all_to_all | solution.py:87
  174.1 147.9 %all-reduce.2.cloned.1.call-done = f32[720,1440]{1,0:T(8,128)} async-done(((f32[720,1440]{1,0:T(8,128)}), f32[720,1440]{1,0:T(8,128)}) %all-reduce.2.cloned.1.call-update) | async-done | bytes 4147216 | tf_op jit(solution)/shard_map/psum | solution.py:95
  322.0 162.3 %while.24 = (s32[]{:T(128)}, f32[4,4096]{1,0:T(4,128)S(1)}, s32[4,4096]{1,0:T(4,128)S(1)}, s32[4,4096]{1,0:T(4,128)S(1)}, f32[720,1440]{1,0:T(8,128)}) while((s32[]{:T(128)}, f32[4,4096]{1,0:T(4,128)S(1)}, s32[4,4096]{1,0:T(4,128)S(1)}, s32[4,4096]{1,0:T(4,128)S(1)}, f32[720,1440]{1,0:T(8,128)}) %tuple.43), condition=%wide.region_3.4_spmd.clone.clone, body=%wide.region_1.3_spmd.clone.sunk.clone | while | flops 17707008 | bytes 70959168 | solution.py:36
  322.1 29.5 %gather_fusion = f32[4096,1440]{1,0:T(8,128)} fusion(f32[720,1440]{1,0:T(8,128)} %get-tuple-element.217, s32[4096]{0:T(1024)S(1)} %broadcast_clamp_fusion.3), kind=kCustom, calls=%fused_computation.clone.clone.1.clone | custom fusion | bytes 47202304 | tf_op jit(solution)/shard_map/while/body/eval_jaxpr/gather | solution.py:33
  351.6 10.8 %select_reduce_fusion.3 = f32[4096]{0:T(1024)S(1)} fusion(f32[4096,1440]{1,0:T(8,128)} %gather_fusion, s32[4096]{0:T(1024)S(1)} %bitcast.201), kind=kLoop, calls=%fused_computation.5.clone.1.clone | loop fusion | flops 17690624 | bytes 23625728 | tf_op jit(solution)/shard_map/while/body/eval_jaxpr/reduce_sum | solution.py:34
  362.6 29.5 %gather_fusion = f32[4096,1440]{1,0:T(8,128)} fusion(f32[720,1440]{1,0:T(8,128)} %get-tuple-element.217, s32[4096]{0:T(1024)S(1)} %broadcast_clamp_fusion.3), kind=kCustom, calls=%fused_computation.clone.clone.1.clone | custom fusion | bytes 47202304 | tf_op jit(solution)/shard_map/while/body/eval_jaxpr/gather | solution.py:33
  392.1 10.8 %select_reduce_fusion.3 = f32[4096]{0:T(1024)S(1)} fusion(f32[4096,1440]{1,0:T(8,128)} %gather_fusion, s32[4096]{0:T(1024)S(1)} %bitcast.201), kind=kLoop, calls=%fused_computation.5.clone.1.clone | loop fusion | flops 17690624 | bytes 23625728 | tf_op jit(solution)/shard_map/while/body/eval_jaxpr/reduce_sum | solution.py:34
  403.2 29.5 %gather_fusion = f32[4096,1440]{1,0:T(8,128)} fusion(f32[720,1440]{1,0:T(8,128)} %get-tuple-element.217, s32[4096]{0:T(1024)S(1)} %broadcast_clamp_fusion.3), kind=kCustom, calls=%fused_computation.clone.clone.1.clone | custom fusion | bytes 47202304 | tf_op jit(solution)/shard_map/while/body/eval_jaxpr/gather | solution.py:33
  432.7 10.8 %select_reduce_fusion.3 = f32[4096]{0:T(1024)S(1)} fusion(f32[4096,1440]{1,0:T(8,128)} %gather_fusion, s32[4096]{0:T(1024)S(1)} %bitcast.201), kind=kLoop, calls=%fused_computation.5.clone.1.clone | loop fusion | flops 17690624 | bytes 23625728 | tf_op jit(solution)/shard_map/while/body/eval_jaxpr/reduce_sum | solution.py:34
  443.8 29.5 %gather_fusion = f32[4096,1440]{1,0:T(8,128)} fusion(f32[720,1440]{1,0:T(8,128)} %get-tuple-element.217, s32[4096]{0:T(1024)S(1)} %broadcast_clamp_fusion.3), kind=kCustom, calls=%fused_computation.clone.clone.1.clone | custom fusion | bytes 47202304 | tf_op jit(solution)/shard_map/while/body/eval_jaxpr/gather | solution.py:33
  473.3 10.8 %select_reduce_fusion.3 = f32[4096]{0:T(1024)S(1)} fusion(f32[4096,1440]{1,0:T(8,128)} %gather_fusion, s32[4096]{0:T(1024)S(1)} %bitcast.201), kind=kLoop, calls=%fused_computation.5.clone.1.clone | loop fusion | flops 17690624 | bytes 23625728 | tf_op jit(solution)/shard_map/while/body/eval_jaxpr/reduce_sum | solution.py:34
  487.0 188.7 %while.25 = (s32[]{:T(128)}, f32[720,1440]{1,0:T(8,128)}, s32[4,4096]{1,0:T(4,128)S(1)}, s32[4,4096]{1,0:T(4,128)S(1)}, f32[4,4096]{1,0:T(4,128)S(1)}) while((s32[]{:T(128)}, f32[720,1440]{1,0:T(8,128)}, s32[4,4096]{1,0:T(4,128)S(1)}, s32[4,4096]{1,0:T(4,128)S(1)}, f32[4,4096]{1,0:T(4,128)S(1)}) %tuple.52), condition=%wide.region_6.7_spmd.clone.clone, body=%wide.region_4.6_spmd.clone.sunk.clone | while | flops 17707008 | bytes 4278857 | solution.py:52
  487.1 47.1 %scatter_custom_fusion.8 = f32[720,1440]{1,0:T(8,128)} fusion(f32[720,1440]{1,0:T(8,128)} %get-tuple-element.224, s32[4096]{0:T(1024)S(1)} %bitcast.203, f32[]{:T(128)} %constant.35.clone.1..sunk.1, f32[4096]{0:T(1024)S(1)} %bitcast.199, s32[4096]{0:T(1024)S(1)} %bitcast.200), kind=kCustom, calls=%fused_computation.10.clone.1.clone | custom fusion | flops 17694720 | bytes 4180480 | tf_op jit(solution)/shard_map/while/body/eval_jaxpr/scatter-add | solution.py:48
  534.3 47.1 %scatter_custom_fusion.8 = f32[720,1440]{1,0:T(8,128)} fusion(f32[720,1440]{1,0:T(8,128)} %get-tuple-element.224, s32[4096]{0:T(1024)S(1)} %bitcast.203, f32[]{:T(128)} %constant.35.clone.1..sunk.1, f32[4096]{0:T(1024)S(1)} %bitcast.199, s32[4096]{0:T(1024)S(1)} %bitcast.200), kind=kCustom, calls=%fused_computation.10.clone.1.clone | custom fusion | flops 17694720 | bytes 4180480 | tf_op jit(solution)/shard_map/while/body/eval_jaxpr/scatter-add | solution.py:48
  581.4 47.1 %scatter_custom_fusion.8 = f32[720,1440]{1,0:T(8,128)} fusion(f32[720,1440]{1,0:T(8,128)} %get-tuple-element.224, s32[4096]{0:T(1024)S(1)} %bitcast.203, f32[]{:T(128)} %constant.35.clone.1..sunk.1, f32[4096]{0:T(1024)S(1)} %bitcast.199, s32[4096]{0:T(1024)S(1)} %bitcast.200), kind=kCustom, calls=%fused_computation.10.clone.1.clone | custom fusion | flops 17694720 | bytes 4180480 | tf_op jit(solution)/shard_map/while/body/eval_jaxpr/scatter-add | solution.py:48
  628.6 47.1 %scatter_custom_fusion.8 = f32[720,1440]{1,0:T(8,128)} fusion(f32[720,1440]{1,0:T(8,128)} %get-tuple-element.224, s32[4096]{0:T(1024)S(1)} %bitcast.203, f32[]{:T(128)} %constant.35.clone.1..sunk.1, f32[4096]{0:T(1024)S(1)} %bitcast.199, s32[4096]{0:T(1024)S(1)} %bitcast.200), kind=kCustom, calls=%fused_computation.10.clone.1.clone | custom fusion | flops 17694720 | bytes 4180480 | tf_op jit(solution)/shard_map/while/body/eval_jaxpr/scatter-add | solution.py:48
  701.2 12.1 %copy.68 = f32[1,1,720,1440]{2,3,0,1:T(8,128)} copy(f32[1,1,720,1440]{3,0,2,1:T(1,128)} %reshape.403) | data formatting | bytes 8294400 | tf_op jit(solution)/shard_map/convert_element_type | solution.py:103
  713.4 32.7 %all-to-all-done.2 = bf16[1,16,45,1440]{3,2,0,1:T(8,128)(2,1)} async-done(((bf16[1,16,45,1440]{3,2,0,1:T(8,128)(2,1)}), bf16[1,16,45,1440]{3,2,0,1:T(8,128)(2,1)}, u32[]{:S(2)}, u32[]{:S(2)}) %all-to-all-start.2) | async-done | bytes 2073632 | tf_op jit(solution)/shard_map/all_to_all | solution.py:101
  749.4 11.7 %fusion.18 = bf16[1,1,720,1440]{2,3,0,1:T(8,128)(2,1)S(1)} fusion(f32[1,1,720,1440]{2,3,0,1:T(8,128)} %copy.68, bf16[720,1440]{1,0:T(8,128)(2,1)} %reshape.400, f32[]{:T(128)} %bitcast.1, f32[]{:T(128)} %bitcast, f32[1440]{0:T(1024)S(1)} %copy-done.13, f32[]{:T(128)} %bitcast.8, f32[]{:T(128)} %bitcast.7, f32[720]{0:T(1024)S(1)} %copy-done.15), kind=kOutput, calls=%fused_computation.31 | convolution fusion | flops 4506969600 | bytes 8303056 | tf_op jit(solution)/shard_map/lab,klbc->klac/dot_general | solution.py:22
  770.9 14.1 %reduce.18 = bf16[720,1440]{1,0:T(8,128)(2,1)S(1)} reduce(bf16[720,1,1,1440]{3,2,1,0:T(2,128)(2,1)} %bitcast.181, bf16[]{:T(256)} %broadcast.349), dimensions={1,2}, to_apply=%bitcast.151.reduce_sub_computation | reduce | bytes 4147202
  790.0 56.5 %all_to_all.36 = bf16[16,2,32400]{2,1,0:T(2,128)(2,1)S(1)} all-to-all(bf16[16,2,32400]{2,1,0:T(2,128)(2,1)} %reshape.460), channel_id=1, replica_groups=mesh['mem'=16,'tile'=16] {'tile'}, dimensions={0} | all-to-all | bytes 4147200 | tf_op jit(solution)/shard_map/all_to_all | solution.py:105
  855.2 15.3 %bitcast_reduce_fusion = bf16[720,1440]{1,0:T(8,128)(2,1)} fusion(bf16[720,1,1,1440]{3,2,1,0:T(2,128)(2,1)} %reshape.461), kind=kLoop, calls=%fused_computation.83 | loop fusion | bytes 4147200 | tf_op jit(solution)/shard_map/all_to_all | solution.py:105
  (115 shorter events, 99.7 us)
Async XLA Ops:
  10.8 9.7 %copy-start.16 = (f32[16]{0:T(128)S(1)}, f32[16]{0:T(128)}, u32[]{:S(2)}) copy-start(f32[16]{0:T(128)} %param.16) | copy-start | bytes 196
  10.8 11.0 %copy-start.17 = (f32[16]{0:T(128)S(1)}, f32[16]{0:T(128)}, u32[]{:S(2)}) copy-start(f32[16]{0:T(128)} %param.17) | copy-start | bytes 196
  10.8 62.6 %all-to-all-start = ((bf16[1,16,45,1440]{3,2,0,1:T(8,128)(2,1)}), bf16[1,16,45,1440]{3,2,0,1:T(8,128)(2,1)S(1)}, u32[]{:S(2)}, u32[]{:S(2)}) async-start(bf16[1,16,45,1440]{3,2,0,1:T(8,128)(2,1)} %copy.50), calls=%async_computation | async-start | bytes 4718592 | tf_op jit(solution)/shard_map/all_to_all | solution.py:84
  20.4 301.6 %all-reduce.2.cloned.1.call-start = ((), (), s32[]{:S(2)}) async-start(), calls=%async_computation.4 | async-start | bytes 8847360 | tf_op jit(solution)/shard_map/psum | solution.py:95
  23.1 65.4 %copy-start.14 = (f32[720]{0:T(1024)}, f32[720]{0:T(1024)S(1)}, u32[]{:S(2)}) copy-start(f32[720]{0:T(1024)S(1)} %iota_convert_fusion.1) | copy-start | bytes 8644
  23.1 65.4 %copy-start.12 = (f32[1440]{0:T(1024)}, f32[1440]{0:T(1024)S(1)}, u32[]{:S(2)}) copy-start(f32[1440]{0:T(1024)S(1)} %iota_convert_fusion) | copy-start | bytes 17284
  73.4 15.1 %copy-start = (bf16[1,16,45,1440]{3,2,0,1:T(8,128)(2,1)}, bf16[1,16,45,1440]{3,2,0,1:T(8,128)(2,1)S(1)}, u32[]{:S(2)}) copy-start(bf16[1,16,45,1440]{3,2,0,1:T(8,128)(2,1)S(1)} %all-to-all-done) | copy-start | bytes 6220804
  88.5 7.8 copy-start.4
  96.7 63.5 %copy-start.2 = (bf16[1,16,45,1440]{3,1,2,0:T(8,128)(2,1)S(1)}, bf16[1,16,45,1440]{3,1,2,0:T(8,128)(2,1)}, u32[]{:S(2)}) copy-start(bf16[1,16,45,1440]{3,1,2,0:T(8,128)(2,1)} %param.15) | copy-start | bytes 6220804
  167.9 0.8 copy-start.9
  167.9 1.7 copy-start.7
  167.9 1.7 copy-start.8
  167.9 2.5 copy-start.10
  167.9 4.0 copy-start.11
  322.0 162.3 %copy-start.5 = (f32[4,4096]{1,0:T(4,128)S(1)}, f32[4,4096]{1,0:T(4,128)}, u32[]{:S(2)}) copy-start(f32[4,4096]{1,0:T(4,128)} %squeeze.23) | copy-start | bytes 196612
  322.0 162.3 %copy-start.6 = (f32[4,4096]{1,0:T(4,128)S(1)}, f32[4,4096]{1,0:T(4,128)}, u32[]{:S(2)}) copy-start(f32[4,4096]{1,0:T(4,128)} %squeeze.24) | copy-start | bytes 196612
  675.7 4.2 copy-start.3
  685.1 8.9 %copy-start.1 = (bf16[1,16,45,1440]{3,2,0,1:T(8,128)(2,1)S(1)}, bf16[1,16,45,1440]{3,2,0,1:T(8,128)(2,1)}, u32[]{:S(2)}) copy-start(bf16[1,16,45,1440]{3,2,0,1:T(8,128)(2,1)} %copy-done) | copy-start | bytes 6220804
  685.1 60.9 %all-to-all-start.2 = ((bf16[1,16,45,1440]{3,2,0,1:T(8,128)(2,1)}), bf16[1,16,45,1440]{3,2,0,1:T(8,128)(2,1)}, u32[]{:S(2)}, u32[]{:S(2)}) async-start(bf16[1,16,45,1440]{3,2,0,1:T(8,128)(2,1)} %fusion.35), calls=%async_computation.2 | async-start | bytes 4718592 | tf_op jit(solution)/shard_map/all_to_all | solution.py:101
  713.4 36.0 %copy-start.13 = (f32[1440]{0:T(1024)S(1)}, f32[1440]{0:T(1024)}, u32[]{:S(2)}) copy-start(f32[1440]{0:T(1024)} %copy-done.12) | copy-start | bytes 17284
  713.4 36.0 %copy-start.15 = (f32[720]{0:T(1024)S(1)}, f32[720]{0:T(1024)}, u32[]{:S(2)}) copy-start(f32[720]{0:T(1024)} %copy-done.14) | copy-start | bytes 8644
Sparse Core Ops, SparseCore 0:
  168.1 153.8 all-reduce.1
